TPU v7x, 32 devices: a whole 2x2x4 slice. The times are simulated.
32 devices in a mesh: row: 4 (over z), col: 8 (over y, x, core).
Axes of the slice: x: 2, y: 2, z: 4, core: 2. Of those that a mesh axis runs over, the one named last changes fastest.
Arguments:
- a_matrix: float32 [16384, 16384], P('row', 'col'), may hold values from -2.25 to 2.25
- b_matrix: float32 [16384, 16384], P('row', 'col'), may hold values from -0.1 to 3.1
- x_block: float32 [16384, 64], P('row'), may hold values from -6 to 6
- r_block: float32 [16384, 64], P('row'), may hold values from -6 to 6
- p_block: float32 [16384, 64], P('row'), may hold values from -6 to 6
Outputs:
- x_next: float32 [16384, 64], P('row')
- r_next: float32 [16384, 64], P('row')
- p_next: float32 [16384, 64], P('row')
All inputs are finite; a program needn't handle non-finite values.
Results may differ from a plain program's by a relative error of at most 0.0003.
Values sent between devices are 32-bit elements; how exact they have to be, the bound alone decides.
A program may use at most 192 MiB of HBM per device.

v0:
```python
import math
import jax
import jax.numpy as jnp
from jax import lax
from jax.sharding import PartitionSpec as P

N = 16384
ITERS = 2
NS_STEPS = 8


def spread(value, axis, source):
    kept = jnp.where(lax.axis_index(axis) == source, value, 0).astype(value.dtype)
    return lax.psum(kept, axis)


def matmul(left, right):
    return jnp.dot(left, right, precision=lax.Precision.HIGHEST, preferred_element_type=jnp.float32)


def ritz_step(gram_a, gram_b, count):
    gram_a = 0.5 * (gram_a + gram_a.T)
    gram_b = 0.5 * (gram_b + gram_b.T)
    lower = jnp.linalg.cholesky(gram_b)
    half = lax.linalg.triangular_solve(lower, gram_a, left_side=True, lower=True)
    middle = lax.linalg.triangular_solve(lower, half.T, left_side=True, lower=True)
    middle = 0.5 * (middle + middle.T)
    extent = middle.shape[0]
    ident = jnp.eye(extent, dtype=middle.dtype)
    shift = jnp.trace(middle) / extent
    centred = middle - shift * ident
    sign_est = centred / jnp.sqrt(jnp.sum(centred * centred) + 1e-06)
    for turn in range(NS_STEPS):
        sign_est = 1.5 * sign_est - 0.5 * matmul(sign_est, matmul(sign_est, sign_est))
    filtered = (0.5 * (ident - sign_est))[:, :count]
    coords = lax.linalg.triangular_solve(
        lower, filtered, left_side=True, lower=True, transpose_a=True
    ) * math.sqrt(N)
    reduced = matmul(filtered.T, matmul(middle, filtered))
    return (coords, reduced)


def local(a_matrix, b_matrix, x_block, r_block, p_block):
    ratio = lax.axis_size("col") // lax.axis_size("row")
    col_index = lax.axis_index("col")
    tile_cols = a_matrix.shape[1]
    width = x_block.shape[1]
    for turn in range(ITERS):
        panel = jnp.concatenate([x_block, r_block, p_block], axis=1)
        own_part = lax.dynamic_slice_in_dim(panel, col_index % ratio * tile_cols, tile_cols, 0)
        matched = spread(own_part, "row", col_index // ratio)
        products = lax.psum(
            jnp.concatenate([matmul(a_matrix, matched), matmul(b_matrix, matched)], axis=1), "col"
        )
        grams = lax.psum(matmul(panel.T, products), "row")
        coords, reduced = ritz_step(grams[:, : 3 * width], grams[:, 3 * width :], width)
        new_resid = matmul(products[:, : 3 * width], coords) - matmul(
            matmul(products[:, 3 * width :], coords), reduced
        )
        x_block = matmul(panel, coords)
        p_block = matmul(panel[:, width:], coords[width:])
        r_block = new_resid
    return (x_block, r_block, p_block)


def solution(mesh):
    return jax.shard_map(
        local,
        mesh=mesh,
        in_specs=(P("row", "col"), P("row", "col"), P("row", None), P("row", None), P("row", None)),
        out_specs=(P("row", None), P("row", None), P("row", None)),
        check_vma=False,
    )
```

profile of v0, /device:TPU:0, one launch (start us, length us, event | category | flops | bytes accessed | tf_op | source)
XLA Modules:
  0.0 861.8 jit_solution(8819377317058890777)
XLA Ops:
  12.5 71.8 %all-reduce.12.cloned.1.call-done = f32[2048,192]{0,1:T(8,128)} async-done(((f32[2048,192]{0,1:T(8,128)}), f32[2048,192]{0,1:T(8,128)}) %all-reduce.12.cloned.1.call-update) | async-done | bytes 1572880 | tf_op jit(solution)/shard_map/psum | solution.py:14
  84.3 40.1 %convolution_bitcast_fusion.2 = f32[4096,192]{0,1:T(8,128)S(1)} fusion(f32[2048,192]{0,1:T(8,128)} %all-reduce.12.cloned.1.call-done, f32[4096,2048]{1,0:T(8,128)} %param.11), kind=kOutput, calls=%fused_computation.4 | convolution fusion | flops 19327352832 | bytes 38273024 | tf_op jit(solution)/shard_map/dot_general | solution.py:18
  124.4 37.8 %convolution_bitcast_fusion.3 = f32[4096,192]{0,1:T(8,128)S(1)} fusion(f32[2048,192]{0,1:T(8,128)S(1)} %copy-done.2, f32[4096,2048]{1,0:T(8,128)} %param.10), kind=kOutput, calls=%fused_computation.5 | convolution fusion | flops 19327352832 | bytes 38273024 | tf_op jit(solution)/shard_map/dot_general | solution.py:18
  162.2 3.1 pad_maximum_fusion
  165.3 103.2 %all-reduce.14.cloned.1.call-done = f32[4096,384]{0,1:T(8,128)} async-done(((f32[4096,384]{0,1:T(8,128)}), f32[4096,384]{0,1:T(8,128)}) %all-reduce.14.cloned.1.call-update) | async-done | bytes 6291472 | tf_op jit(solution)/shard_map/psum | solution.py:52
  268.5 9.2 %fusion.104 = f32[192,384]{1,0:T(8,128)} fusion(f32[4096,192]{0,1:T(8,128)S(1)} %constant_dynamic-update-slice_fusion, f32[4096,384]{0,1:T(8,128)} %all-reduce.14.cloned.1.call-done), kind=kOutput, calls=%fused_computation.191 | convolution fusion | flops 3623878656 | bytes 9732096 | tf_op jit(solution)/shard_map/dot_general | solution.py:18
  278.0 35.9 %all-reduce.16.cloned.1.call-done = f32[192,384]{1,0:T(8,128)} async-done(((f32[192,384]{1,0:T(8,128)}), f32[192,384]{1,0:T(8,128)}) %all-reduce.16.cloned.1.call-update) | async-done | bytes 294928 | tf_op jit(solution)/shard_map/psum | solution.py:55
  317.4 1.9 fusion.42
  325.0 13.2 %cholesky.136 = f32[128,128]{1,0:T(8,128)} custom-call(f32[128,128]{1,0:T(8,128)} %copy.11), custom_call_target="Cholesky" | custom-call | tf_op jit(solution)/shard_map/jit(cholesky)/cholesky | solution.py:24
  341.2 11.3 %custom-call.19 = f32[1,128,128]{1,2,0:T(8,128)} custom-call(f32[1,128,128]{2,1,0:T(8,128)} %get-tuple-element.81), custom_call_target="InvertDiagBlocksLowerTriangular" | custom-call | tf_op jit(solution)/shard_map/jit(cholesky)/cholesky | solution.py:24
  357.2 6.6 cholesky.156
  369.4 21.5 %custom-call.22 = f32[2,128,128]{1,2,0:T(8,128)} custom-call(f32[2,128,128]{2,1,0:T(8,128)} %pad_maximum_fusion.5), custom_call_target="InvertDiagBlocksLowerTriangular" | custom-call | tf_op jit(solution)/shard_map/triangular_solve/custom-call.4 | solution.py:36
  417.2 2.2 fusion.100
  421.2 7.0 fusion.4
  428.2 2.2 fusion.6
  430.4 2.5 convolution_subtract_fusion.1
  434.5 68.8 %all-reduce.18.cloned.1.call-done = f32[2048,192]{0,1:T(8,128)} async-done(((f32[2048,192]{0,1:T(8,128)}), f32[2048,192]{0,1:T(8,128)}) %all-reduce.18.cloned.1.call-update) | async-done | bytes 1572880 | tf_op jit(solution)/shard_map/psum | solution.py:14
  503.4 40.5 %convolution_bitcast_fusion = f32[4096,192]{0,1:T(8,128)S(1)} fusion(f32[2048,192]{0,1:T(8,128)} %all-reduce.18.cloned.1.call-done, f32[4096,2048]{1,0:T(8,128)} %param.11), kind=kOutput, calls=%fused_computation.2 | convolution fusion | flops 19327352832 | bytes 38273024 | tf_op jit(solution)/shard_map/dot_general | solution.py:18
  543.9 37.6 %convolution_bitcast_fusion.1 = f32[4096,192]{0,1:T(8,128)S(1)} fusion(f32[2048,192]{0,1:T(8,128)S(1)} %copy-done.3, f32[4096,2048]{1,0:T(8,128)} %param.10), kind=kOutput, calls=%fused_computation.3 | convolution fusion | flops 19327352832 | bytes 38273024 | tf_op jit(solution)/shard_map/dot_general | solution.py:18
  581.4 3.1 pad_maximum_fusion.1
  584.6 103.2 %all-reduce.20.cloned.1.call-done = f32[4096,384]{0,1:T(8,128)} async-done(((f32[4096,384]{0,1:T(8,128)}), f32[4096,384]{0,1:T(8,128)}) %all-reduce.20.cloned.1.call-update) | async-done | bytes 6291472 | tf_op jit(solution)/shard_map/psum | solution.py:52
  687.8 9.3 %fusion.101 = f32[192,384]{1,0:T(8,128)} fusion(f32[4096,384]{0,1:T(8,128)} %all-reduce.20.cloned.1.call-done, f32[4096,64]{0,1:T(8,128)S(1)} %fusion.8, f32[4096,64]{0,1:T(8,128)S(1)} %convolution_subtract_fusion.1, f32[4096,64]{0,1:T(8,128)S(1)} %copy-done.1), kind=kOutput, calls=%fused_computation.190 | convolution fusion | flops 3625451520 | bytes 9732096 | tf_op jit(solution)/shard_map/dot_general | solution.py:18
  697.1 36.2 %all-reduce.22.cloned.1.call-done = f32[192,384]{1,0:T(8,128)} async-done(((f32[192,384]{1,0:T(8,128)}), f32[192,384]{1,0:T(8,128)}) %all-reduce.22.cloned.1.call-update) | async-done | bytes 294928 | tf_op jit(solution)/shard_map/psum | solution.py:55
  746.2 13.2 %cholesky.174 = f32[128,128]{1,0:T(8,128)} custom-call(f32[128,128]{1,0:T(8,128)} %cholesky.211), custom_call_target="Cholesky" | custom-call | tf_op jit(solution)/shard_map/jit(cholesky)/cholesky | solution.py:24
  762.4 11.3 %custom-call.23 = f32[1,128,128]{1,2,0:T(8,128)} custom-call(f32[1,128,128]{2,1,0:T(8,128)} %get-tuple-element.79), custom_call_target="InvertDiagBlocksLowerTriangular" | custom-call | tf_op jit(solution)/shard_map/jit(cholesky)/cholesky | solution.py:24
  776.8 6.6 cholesky.194
  789.0 21.3 %custom-call.26 = f32[2,128,128]{1,2,0:T(8,128)} custom-call(f32[2,128,128]{2,1,0:T(8,128)} %pad_maximum_fusion.6), custom_call_target="InvertDiagBlocksLowerTriangular" | custom-call | tf_op jit(solution)/shard_map/triangular_solve/custom-call.4 | solution.py:36
  836.0 3.1 fusion.99
  839.2 2.7 fusion.12
  842.2 7.0 fusion
  849.1 2.2 fusion.2
  851.3 3.5 convolution_subtract_fusion
  (175 shorter events, 102.7 us)
Async XLA Ops:
  7.2 77.1 %all-reduce.12.cloned.1.call-start = ((), (), s32[]{:S(2)}) async-start(), calls=%async_computation | async-start | bytes 3145728 | tf_op jit(solution)/shard_map/psum | solution.py:14
  12.5 256.0 %all-reduce.14.cloned.1.call-start = ((), (), s32[]{:S(2)}) async-start(), calls=%async_computation.1 | async-start | bytes 12582912 | tf_op jit(solution)/shard_map/psum | solution.py:52
  84.3 40.1 %copy-start.2 = (f32[2048,192]{0,1:T(8,128)S(1)}, f32[2048,192]{0,1:T(8,128)}, u32[]{:S(2)}) copy-start(f32[2048,192]{0,1:T(8,128)} %all-reduce.12.cloned.1.call-done) | copy-start | bytes 4718596
  165.3 148.6 %all-reduce.16.cloned.1.call-start = ((), (), s32[]{:S(2)}) async-start(), calls=%async_computation.2 | async-start | bytes 589824 | tf_op jit(solution)/shard_map/psum | solution.py:55
  277.7 225.6 %all-reduce.18.cloned.1.call-start = ((), (), s32[]{:S(2)}) async-start(), calls=%async_computation.3 | async-start | bytes 3145728 | tf_op jit(solution)/shard_map/psum | solution.py:14
  313.9 78.7 %copy-start.6 = (f32[192,384]{1,0:T(8,128)S(1)}, f32[192,384]{1,0:T(8,128)}, u32[]{:S(2)}) copy-start(f32[192,384]{1,0:T(8,128)} %all-reduce.16.cloned.1.call-done) | copy-start | bytes 884740
  322.1 0.7 copy-start.14
  368.0 0.7 copy-start.9
  396.7 0.7 copy-start.10
  400.9 0.6 copy-start.15
  408.8 6.5 copy-start.13
  412.3 8.9 %slice-start = ((s8[6291456]{0:T(1024)(128)(4,1)}), s8[4194304]{0:T(1024)(128)(4,1)S(1)}, s32[]{:S(2)}) async-start(s8[6291456]{0:T(1024)(128)(4,1)} %bitcast.196), calls=%async_computation.6 | async-start | bytes 8388608
  414.1 5.6 copy-start.4
  414.1 5.6 copy-start.5
  417.2 4.0 slice-start.1
  419.4 13.5 %copy-start = (f32[4096,64]{0,1:T(8,128)}, f32[4096,64]{0,1:T(8,128)S(1)}, u32[]{:S(2)}) copy-start(f32[4096,64]{0,1:T(8,128)S(1)} %fusion.100) | copy-start | bytes 3145732
  434.5 253.3 %all-reduce.20.cloned.1.call-start = ((), (), s32[]{:S(2)}) async-start(), calls=%async_computation.4 | async-start | bytes 12582912 | tf_op jit(solution)/shard_map/psum | solution.py:52
  503.4 40.5 %copy-start.3 = (f32[2048,192]{0,1:T(8,128)S(1)}, f32[2048,192]{0,1:T(8,128)}, u32[]{:S(2)}) copy-start(f32[2048,192]{0,1:T(8,128)} %all-reduce.18.cloned.1.call-done) | copy-start | bytes 4718596
  584.5 103.3 %copy-start.1 = (f32[4096,64]{0,1:T(8,128)S(1)}, f32[4096,64]{0,1:T(8,128)}, u32[]{:S(2)}) copy-start(f32[4096,64]{0,1:T(8,128)} %copy-done) | copy-start | bytes 3145732
  584.5 148.8 %all-reduce.22.cloned.1.call-start = ((), (), s32[]{:S(2)}) async-start(), calls=%async_computation.5 | async-start | bytes 589824 | tf_op jit(solution)/shard_map/psum | solution.py:55
  733.3 78.7 %copy-start.7 = (f32[192,384]{1,0:T(8,128)S(1)}, f32[192,384]{1,0:T(8,128)}, u32[]{:S(2)}) copy-start(f32[192,384]{1,0:T(8,128)} %all-reduce.22.cloned.1.call-done) | copy-start | bytes 884740
  744.9 0.7 copy-start.16
  787.6 0.7 copy-start.8
  816.1 0.7 copy-start.11
  827.6 6.4 copy-start.12
  831.1 11.0 %slice-start.2 = ((s8[6291456]{0:T(1024)(128)(4,1)}), s8[4194304]{0:T(1024)(128)(4,1)S(1)}, s32[]{:S(2)}) async-start(s8[6291456]{0:T(1024)(128)(4,1)} %bitcast.198), calls=%async_computation.8 | async-start | bytes 8388608
  836.0 6.1 slice-start.3
Sparse Core Ops, SparseCore 0:
  12.6 71.6 all-reduce.11
  165.4 103.0 all-reduce.13
  277.8 36.0 all-reduce.15
  434.6 68.7 all-reduce.17
  584.7 103.0 all-reduce.19
  697.3 36.0 all-reduce.21
where the time goes:
time: 870 us; the launch traced here: 862 us
  waiting for transfers between devices  419 us (48%)
  matrix products  251 us (29%)
  other arithmetic  138 us (16%)
  local copies, waits for them, and re-layouts  33.3 us (4%)
  between operations  20.3 us (2%)
    dot_general x52, matrix products, matmul(): jnp.dot(left, right, precision=lax.Precision.HIGHEST, preferred_element_t...  228 us
    psum x2, waiting for transfers between devices, local(): lax.psum(jnp.concatenate([matmul(a_matrix, matched), matmul(b_matrix, mat...  206 us
    psum x2, waiting for transfers between devices, spread(): return lax.psum(kept, axis)  141 us
    psum x2, waiting for transfers between devices, local(): grams = lax.psum(matmul(panel.T, products), 'row')  72.1 us
    another operation x14, other arithmetic, ritz_step(): lower = jnp.linalg.cholesky(gram_b)  68.9 us
    another operation x10, other arithmetic, ritz_step(): lax.linalg.triangular_solve(lower, filtered, left_side=True, lower=True,...  46.2 us
  transfers between devices with their start and end apart: 6, of which 6 were waited for; matrix products, arithmetic and copies ran while one was open for 0% of the time, Pallas kernels for 0%

commit v1 on v0

--- a/solution.py
+++ b/solution.py
@@ -52,7 +52,9 @@
         products = lax.psum(
             jnp.concatenate([matmul(a_matrix, matched), matmul(b_matrix, matched)], axis=1), "col"
         )
-        grams = lax.psum(matmul(panel.T, products), "row")
+        own = matmul(panel.T, products)
+        parts = lax.all_gather(own, "row")
+        grams = jnp.sum(parts, axis=0)
         coords, reduced = ritz_step(grams[:, : 3 * width], grams[:, 3 * width :], width)
         new_resid = matmul(products[:, : 3 * width], coords) - matmul(
             matmul(products[:, 3 * width :], coords), reduced

time: 870 us -> 858 us (0.986)
  waiting for transfers between devices: 419 us -> 407 us
    psum x2 -> x0, waiting for transfers between devices: 72.1 us -> none  [local(): grams = lax.psum(matmul(panel.T, products), 'row')]
    all_gather x0 -> x2, waiting for transfers between devices: none -> 60.7 us  [local(): parts = lax.all_gather(own, 'row')]
where the time goes in v1:
time: 858 us; the launch traced here: 850 us
  waiting for transfers between devices  407 us (47%)
  matrix products  251 us (29%)
  other arithmetic  140 us (16%)
  local copies, waits for them, and re-layouts  31.3 us (4%)
  between operations  20.1 us (2%)
    dot_general x52, matrix products, matmul(): jnp.dot(left, right, precision=lax.Precision.HIGHEST, preferred_element_t...  228 us
    psum x2, waiting for transfers between devices, local(): lax.psum(jnp.concatenate([matmul(a_matrix, matched), matmul(b_matrix, mat...  206 us
    psum x2, waiting for transfers between devices, spread(): return lax.psum(kept, axis)  140 us
    another operation x14, other arithmetic, ritz_step(): lower = jnp.linalg.cholesky(gram_b)  68.8 us
    all_gather x2, waiting for transfers between devices, local(): parts = lax.all_gather(own, 'row')  60.7 us
    another operation x10, other arithmetic, ritz_step(): lax.linalg.triangular_solve(lower, filtered, left_side=True, lower=True,...  46.2 us
  transfers between devices with their start and end apart: 6, of which 6 were waited for; matrix products, arithmetic and copies ran while one was open for 0% of the time, Pallas kernels for 0%

profile of v1, /device:TPU:0, one launch (start us, length us, event | category | flops | bytes accessed | tf_op | source)
XLA Modules:
  0.0 850.0 jit_solution(4971815525246599657)
XLA Ops:
  12.5 71.8 %all-reduce.10.cloned.1.call-done = f32[2048,192]{0,1:T(8,128)} async-done(((f32[2048,192]{0,1:T(8,128)}), f32[2048,192]{0,1:T(8,128)}) %all-reduce.10.cloned.1.call-update) | async-done | bytes 1572880 | tf_op jit(solution)/shard_map/psum | solution.py:14
  84.3 40.1 %convolution_bitcast_fusion.2 = f32[4096,192]{0,1:T(8,128)S(1)} fusion(f32[2048,192]{0,1:T(8,128)} %all-reduce.10.cloned.1.call-done, f32[4096,2048]{1,0:T(8,128)} %param.11), kind=kOutput, calls=%fused_computation.4 | convolution fusion | flops 19327352832 | bytes 38273024 | tf_op jit(solution)/shard_map/dot_general | solution.py:18
  124.4 37.8 %convolution_bitcast_fusion.3 = f32[4096,192]{0,1:T(8,128)S(1)} fusion(f32[2048,192]{0,1:T(8,128)S(1)} %copy-done.2, f32[4096,2048]{1,0:T(8,128)} %param.10), kind=kOutput, calls=%fused_computation.5 | convolution fusion | flops 19327352832 | bytes 38273024 | tf_op jit(solution)/shard_map/dot_general | solution.py:18
  162.2 3.1 pad_maximum_fusion
  165.3 103.2 %all-reduce.12.cloned.1.call-done = f32[4096,384]{0,1:T(8,128)} async-done(((f32[4096,384]{0,1:T(8,128)}), f32[4096,384]{0,1:T(8,128)}) %all-reduce.12.cloned.1.call-update) | async-done | bytes 6291472 | tf_op jit(solution)/shard_map/psum | solution.py:52
  268.5 9.2 %fusion.104 = f32[192,384]{1,0:T(8,128)} fusion(f32[4096,192]{0,1:T(8,128)S(1)} %constant_dynamic-update-slice_fusion, f32[4096,384]{0,1:T(8,128)} %all-reduce.12.cloned.1.call-done), kind=kOutput, calls=%fused_computation.191 | convolution fusion | flops 3623878656 | bytes 9732096 | tf_op jit(solution)/shard_map/dot_general | solution.py:18
  278.0 30.2 %all-gather.5.cloned.1.call-done = f32[768,384]{1,0:T(8,128)} async-done(((f32[192,384]{1,0:T(8,128)}), f32[768,384]{1,0:T(8,128)}) %all-gather.5.cloned.1.call-update) | async-done | bytes 1179664 | tf_op jit(solution)/shard_map/all_gather | solution.py:56
  319.5 13.2 %cholesky.136 = f32[128,128]{1,0:T(8,128)} custom-call(f32[128,128]{1,0:T(8,128)} %copy.11), custom_call_target="Cholesky" | custom-call | tf_op jit(solution)/shard_map/jit(cholesky)/cholesky | solution.py:24
  335.6 11.3 %custom-call.19 = f32[1,128,128]{1,2,0:T(8,128)} custom-call(f32[1,128,128]{2,1,0:T(8,128)} %get-tuple-element.81), custom_call_target="InvertDiagBlocksLowerTriangular" | custom-call | tf_op jit(solution)/shard_map/jit(cholesky)/cholesky | solution.py:24
  346.9 1.8 constant_dynamic-update-slice_fusion.6
  351.7 6.6 cholesky.156
  363.8 21.5 %custom-call.22 = f32[2,128,128]{1,2,0:T(8,128)} custom-call(f32[2,128,128]{2,1,0:T(8,128)} %pad_maximum_fusion.5), custom_call_target="InvertDiagBlocksLowerTriangular" | custom-call | tf_op jit(solution)/shard_map/triangular_solve/custom-call.4 | solution.py:36
  411.5 2.2 fusion.100
  415.5 7.0 fusion.4
  422.5 2.2 fusion.6
  424.7 2.5 convolution_subtract_fusion.1
  428.8 68.3 %all-reduce.14.cloned.1.call-done = f32[2048,192]{0,1:T(8,128)} async-done(((f32[2048,192]{0,1:T(8,128)}), f32[2048,192]{0,1:T(8,128)}) %all-reduce.14.cloned.1.call-update) | async-done | bytes 1572880 | tf_op jit(solution)/shard_map/psum | solution.py:14
  497.1 40.5 %convolution_bitcast_fusion = f32[4096,192]{0,1:T(8,128)S(1)} fusion(f32[2048,192]{0,1:T(8,128)} %all-reduce.14.cloned.1.call-done, f32[4096,2048]{1,0:T(8,128)} %param.11), kind=kOutput, calls=%fused_computation.2 | convolution fusion | flops 19327352832 | bytes 38273024 | tf_op jit(solution)/shard_map/dot_general | solution.py:18
  537.6 37.6 %convolution_bitcast_fusion.1 = f32[4096,192]{0,1:T(8,128)S(1)} fusion(f32[2048,192]{0,1:T(8,128)S(1)} %copy-done.3, f32[4096,2048]{1,0:T(8,128)} %param.10), kind=kOutput, calls=%fused_computation.3 | convolution fusion | flops 19327352832 | bytes 38273024 | tf_op jit(solution)/shard_map/dot_general | solution.py:18
  575.2 3.1 pad_maximum_fusion.1
  578.3 103.2 %all-reduce.16.cloned.1.call-done = f32[4096,384]{0,1:T(8,128)} async-done(((f32[4096,384]{0,1:T(8,128)}), f32[4096,384]{0,1:T(8,128)}) %all-reduce.16.cloned.1.call-update) | async-done | bytes 6291472 | tf_op jit(solution)/shard_map/psum | solution.py:52
  681.5 9.4 %fusion.101 = f32[192,384]{1,0:T(8,128)} fusion(f32[4096,384]{0,1:T(8,128)} %all-reduce.16.cloned.1.call-done, f32[4096,64]{0,1:T(8,128)S(1)} %fusion.8, f32[4096,64]{0,1:T(8,128)S(1)} %convolution_subtract_fusion.1, f32[4096,64]{0,1:T(8,128)S(1)} %copy-done.1), kind=kOutput, calls=%fused_computation.190 | convolution fusion | flops 3625451520 | bytes 9732096 | tf_op jit(solution)/shard_map/dot_general | solution.py:18
  690.9 30.5 %all-gather.7.cloned.1.call-done = f32[768,384]{1,0:T(8,128)} async-done(((f32[192,384]{1,0:T(8,128)}), f32[768,384]{1,0:T(8,128)}) %all-gather.7.cloned.1.call-update) | async-done | bytes 1179664 | tf_op jit(solution)/shard_map/all_gather | solution.py:56
  734.4 13.2 %cholesky.174 = f32[128,128]{1,0:T(8,128)} custom-call(f32[128,128]{1,0:T(8,128)} %cholesky.211), custom_call_target="Cholesky" | custom-call | tf_op jit(solution)/shard_map/jit(cholesky)/cholesky | solution.py:24
  750.6 11.3 %custom-call.23 = f32[1,128,128]{1,2,0:T(8,128)} custom-call(f32[1,128,128]{2,1,0:T(8,128)} %get-tuple-element.79), custom_call_target="InvertDiagBlocksLowerTriangular" | custom-call | tf_op jit(solution)/shard_map/jit(cholesky)/cholesky | solution.py:24
  765.1 6.6 cholesky.194
  777.2 21.3 %custom-call.26 = f32[2,128,128]{1,2,0:T(8,128)} custom-call(f32[2,128,128]{2,1,0:T(8,128)} %pad_maximum_fusion.6), custom_call_target="InvertDiagBlocksLowerTriangular" | custom-call | tf_op jit(solution)/shard_map/triangular_solve/custom-call.4 | solution.py:36
  824.2 3.1 fusion.99
  827.3 2.7 fusion.12
  830.3 7.0 fusion
  837.3 2.2 fusion.2
  839.5 3.5 convolution_subtract_fusion
  (173 shorter events, 103.2 us)
Async XLA Ops:
  7.2 77.1 %all-reduce.10.cloned.1.call-start = ((), (), s32[]{:S(2)}) async-start(), calls=%async_computation | async-start | bytes 3145728 | tf_op jit(solution)/shard_map/psum | solution.py:14
  12.5 256.0 %all-reduce.12.cloned.1.call-start = ((), (), s32[]{:S(2)}) async-start(), calls=%async_computation.1 | async-start | bytes 12582912 | tf_op jit(solution)/shard_map/psum | solution.py:52
  84.3 40.1 %copy-start.2 = (f32[2048,192]{0,1:T(8,128)S(1)}, f32[2048,192]{0,1:T(8,128)}, u32[]{:S(2)}) copy-start(f32[2048,192]{0,1:T(8,128)} %all-reduce.10.cloned.1.call-done) | copy-start | bytes 4718596
  165.2 143.0 %all-gather.5.cloned.1.call-start = ((), (), s32[]{:S(2)}) async-start(), calls=%async_computation.4 | async-start | bytes 1474560 | tf_op jit(solution)/shard_map/all_gather | solution.py:56
  277.7 219.4 %all-reduce.14.cloned.1.call-start = ((), (), s32[]{:S(2)}) async-start(), calls=%async_computation.2 | async-start | bytes 3145728 | tf_op jit(solution)/shard_map/psum | solution.py:14
  316.6 0.7 copy-start.12
  362.4 0.7 copy-start.7
  391.1 0.7 copy-start.8
  395.3 0.6 copy-start.13
  403.1 6.5 copy-start.11
  406.6 8.9 %slice-start = ((s8[6291456]{0:T(1024)(128)(4,1)}), s8[4194304]{0:T(1024)(128)(4,1)S(1)}, s32[]{:S(2)}) async-start(s8[6291456]{0:T(1024)(128)(4,1)} %bitcast.198), calls=%async_computation.6 | async-start | bytes 8388608
  408.3 5.6 copy-start.4
  408.4 5.6 copy-start.5
  411.5 4.0 slice-start.1
  413.7 13.5 %copy-start = (f32[4096,64]{0,1:T(8,128)}, f32[4096,64]{0,1:T(8,128)S(1)}, u32[]{:S(2)}) copy-start(f32[4096,64]{0,1:T(8,128)S(1)} %fusion.100) | copy-start | bytes 3145732
  428.8 252.7 %all-reduce.16.cloned.1.call-start = ((), (), s32[]{:S(2)}) async-start(), calls=%async_computation.3 | async-start | bytes 12582912 | tf_op jit(solution)/shard_map/psum | solution.py:52
  497.1 40.5 %copy-start.3 = (f32[2048,192]{0,1:T(8,128)S(1)}, f32[2048,192]{0,1:T(8,128)}, u32[]{:S(2)}) copy-start(f32[2048,192]{0,1:T(8,128)} %all-reduce.14.cloned.1.call-done) | copy-start | bytes 4718596
  578.2 103.3 %copy-start.1 = (f32[4096,64]{0,1:T(8,128)S(1)}, f32[4096,64]{0,1:T(8,128)}, u32[]{:S(2)}) copy-start(f32[4096,64]{0,1:T(8,128)} %copy-done) | copy-start | bytes 3145732
  578.3 143.1 %all-gather.7.cloned.1.call-start = ((), (), s32[]{:S(2)}) async-start(), calls=%async_computation.5 | async-start | bytes 1474560 | tf_op jit(solution)/shard_map/all_gather | solution.py:56
  733.1 0.7 copy-start.14
  775.8 0.7 copy-start.6
  804.3 0.7 copy-start.9
  815.8 6.4 copy-start.10
  819.3 11.0 %slice-start.2 = ((s8[6291456]{0:T(1024)(128)(4,1)}), s8[4194304]{0:T(1024)(128)(4,1)S(1)}, s32[]{:S(2)}) async-start(s8[6291456]{0:T(1024)(128)(4,1)} %bitcast.200), calls=%async_computation.8 | async-start | bytes 8388608
  824.2 6.1 slice-start.3
Sparse Core Ops, SparseCore 0:
  12.6 71.6 all-reduce.9
  165.4 103.0 all-reduce.11
  277.8 30.3 all-gather.4
  428.9 68.1 all-reduce.13
  578.4 103.0 all-reduce.15
  691.0 30.3 all-gather.6
